TPU v7x, 256 devices: a whole 4x4x8 slice. The times are simulated.
256 devices in a mesh: cp: 8 (over x, z_hi), fsdp: 32 (over z_lo, y, core).
Axes of the slice: x: 4, y: 4, z: 8 (z_hi: 2, z_lo: 4; z = z_hi * 4 + z_lo), core: 2. Of those that a mesh axis runs over, the one named last changes fastest.
Arguments:
- hidden: bfloat16 [32, 1024, 16384], P('fsdp', 'cp'), may hold values from -6 to 6
- norm_gain: bfloat16 [16384], P('fsdp'), may hold values from 0.25 to 1.75
- query_weight: bfloat16 [16384, 256], P('fsdp'), may hold values from -0.0625 to 0.0625
- key_weight: bfloat16 [16384, 128], P('fsdp'), may hold values from -0.0625 to 0.0625
- value_weight: bfloat16 [16384, 128], P('fsdp'), may hold values from -0.046875 to 0.046875
- out_weight: bfloat16 [256, 16384], P(None, 'fsdp'), may hold values from -0.75 to 0.75
- doc_lengths: int32 [32, 4], P('fsdp'), may hold values from 1 to 512, 1024 in all within a row
Outputs:
- attention_out: bfloat16 [32, 1024, 16384], P('fsdp', 'cp')
Inputs may be any that keep to these rules, and one draw needn't show every extreme that they name: `doc_lengths`: each row holds the lengths of the 4 documents of one sequence in order; they sum to 1024 and the longest is exactly 512.
All inputs are finite; a program needn't handle non-finite values.
Results may differ from a plain program's by a relative error of at most 0.012.
Values may be sent and summed in bfloat16 or wider, within the bound.
A program may use at most 128 MiB of HBM per device.

v0:
```python
import math
import jax
import jax.numpy as jnp
from jax import lax
from jax.sharding import PartitionSpec as P

BLK = 128
EPSILON = 1e-05
THETA = 500000.0


def side_by_side(arrays, axis, dim, along):
    columns = [a.reshape(*a.shape[:along], -1) for a in arrays]
    both = jnp.concatenate(columns, axis=along)
    out, at, outs = (lax.all_gather(both, axis, axis=dim, tiled=True), 0, [])
    for a, column in zip(arrays, columns):
        section = out[..., at : at + column.shape[along]]
        outs.append(section.reshape(*section.shape[:along], *a.shape[along:]))
        at += column.shape[along]
    return tuple(outs)


def copy_for_each(array, axis):
    length = lax.axis_size(axis)
    return lax.all_to_all(
        jnp.broadcast_to(array[None], (length, *array.shape)), axis, 0, 0, tiled=True
    )


def laid_out(tiles, dim):
    tiles = jnp.moveaxis(tiles, 0, dim)
    shape = tiles.shape
    return tiles.reshape(*shape[:dim], shape[dim] * shape[dim + 1], *shape[dim + 2 :])


def gathered_copies(array, axis, dim):
    tiles = copy_for_each(array, axis)
    return laid_out(tiles, dim)


def side_by_side_2(arrays, axis, dim, along):
    ends, at = ([], 0)
    for a in arrays[:-1]:
        at += a.shape[along]
        ends.append(at)
    both = jnp.concatenate(arrays, axis=along)
    return tuple(jnp.split(gathered_copies(both, axis, dim), ends, axis=along))


def doc_tables(lengths, total):
    ends = jnp.cumsum(lengths)
    starts = ends - lengths
    places = jnp.arange(total, dtype=jnp.int32)
    after = (ends[None, :] <= places[:, None]).astype(jnp.int32)
    doc_ids = jnp.sum(after, axis=1)
    member = (doc_ids[:, None] == jnp.arange(lengths.shape[0], dtype=jnp.int32)[None, :]).astype(
        jnp.int32
    )
    offsets = places - jnp.sum(member * starts[None, :], axis=1)
    return (doc_ids, offsets)


def rotate(values, offsets):
    head_dim = values.shape[2]
    half = head_dim // 2
    rates = jnp.power(THETA, -2.0 * jnp.arange(half, dtype=jnp.float32) / head_dim)
    angles = offsets.astype(jnp.float32)[:, None] * rates[None, :]
    cosine = jnp.cos(angles)[:, None, :]
    sine = jnp.sin(angles)[:, None, :]
    first = values[:, :, :half]
    second = values[:, :, half:]
    return jnp.concatenate([first * cosine - second * sine, second * cosine + first * sine], axis=2)


def fold_panels(columns, pieces):
    gain_piece, query_piece, key_piece, value_piece = pieces
    normed = (columns * gain_piece.astype(jnp.float32)[None, :]).astype(jnp.bfloat16)
    return (
        jnp.dot(normed, query_piece, preferred_element_type=jnp.float32),
        jnp.dot(normed, key_piece, preferred_element_type=jnp.float32),
        jnp.dot(normed, value_piece, preferred_element_type=jnp.float32),
    )


def keep_same(operand):
    return operand


def attend_blocks(blocks, doc_ids, state, pieces):
    key_rows, value_rows = pieces
    count = key_rows.shape[0]
    tile_size = math.gcd(count, BLK)

    def one_tile(tile_index, inner):
        first = tile_index * tile_size
        key_tile = lax.dynamic_slice_in_dim(key_rows, tile_index * tile_size, tile_size, 0)
        value_tile = lax.dynamic_slice_in_dim(value_rows, tile_index * tile_size, tile_size, 0)
        key_places = first + jnp.arange(tile_size, dtype=jnp.int32)
        key_docs = lax.dynamic_slice_in_dim(doc_ids, first, tile_size, 0)
        updated = []
        for block, carried in zip(blocks, inner):
            queries, query_first = block
            length = queries.shape[1]
            query_docs = lax.dynamic_slice_in_dim(doc_ids, query_first, length, 0)
            query_places = query_first + jnp.arange(length, dtype=jnp.int32)
            live = jnp.logical_and(
                first <= query_first + length - 1, key_docs[tile_size - 1] >= query_docs[0]
            )

            def compute(operand):
                numer, denom = operand
                scores = jnp.einsum(
                    "hqd,kd->hqk", queries, key_tile, preferred_element_type=jnp.float32
                )
                allowed = jnp.logical_and(
                    query_docs[:, None] == key_docs[None, :],
                    key_places[None, :] <= query_places[:, None],
                )
                weights = jnp.where(allowed[None, :, :], jnp.exp(scores), jnp.float32(0.0))
                numer = numer + jnp.einsum(
                    "hqk,kd->hqd",
                    weights.astype(jnp.bfloat16),
                    value_tile,
                    preferred_element_type=jnp.float32,
                )
                return (numer, denom + jnp.sum(weights, axis=2))

            updated.append(lax.cond(live, compute, keep_same, carried))
        return tuple(updated)

    return lax.fori_loop(0, count // tile_size, one_tile, state)


def local(hidden, norm_gain, query_weight, key_weight, value_weight, out_weight, doc_lengths):
    rows = hidden.shape[1]
    head_dim = key_weight.shape[1]
    heads = query_weight.shape[1] // head_dim
    groups = lax.axis_size("cp")
    position = lax.axis_index("cp")
    doc_ids, offsets = doc_tables(doc_lengths[0], rows * groups)
    tokens = hidden[0].astype(jnp.float32)
    scaled = tokens * lax.rsqrt(jnp.mean(tokens * tokens, axis=1, keepdims=True) + EPSILON)
    query_raw, key_raw, value_raw = fold_panels(
        scaled, side_by_side((norm_gain, query_weight, key_weight, value_weight), "fsdp", 0, 1)
    )
    own_offsets = lax.dynamic_slice_in_dim(offsets, position * rows, rows, 0)
    queries = (
        rotate(query_raw.reshape(rows, heads, head_dim), own_offsets) * head_dim ** (-0.5)
    ).astype(jnp.bfloat16)
    queries = queries.transpose(1, 0, 2)
    key_rows = rotate(key_raw.reshape(rows, 1, head_dim), own_offsets)[:, 0, :].astype(jnp.bfloat16)
    value_rows = value_raw.astype(jnp.bfloat16)
    blocks = ((queries, position * rows),)
    start_state = tuple(
        (
            (
                jnp.zeros((heads, block[0].shape[1], head_dim), jnp.float32),
                jnp.zeros((heads, block[0].shape[1]), jnp.float32),
            )
            for block in blocks
        )
    )
    state = attend_blocks(
        blocks, doc_ids, start_state, side_by_side_2((key_rows, value_rows), "cp", 0, 1)
    )
    results = [
        (numer / denom[:, :, None])
        .astype(jnp.bfloat16)
        .transpose(1, 0, 2)
        .reshape(numer.shape[1], heads * head_dim)
        for numer, denom in state
    ]
    attended = results[0]
    mixed = jnp.dot(
        attended,
        lax.all_gather(out_weight, "fsdp", axis=1, tiled=True),
        preferred_element_type=jnp.float32,
    ).astype(jnp.bfloat16)
    return mixed[None, :, :]


def solution(mesh):
    in_specs = (
        P("fsdp", "cp", None),
        P("fsdp"),
        P("fsdp", None),
        P("fsdp", None),
        P("fsdp", None),
        P(None, "fsdp"),
        P("fsdp", None),
    )
    out_specs = P("fsdp", "cp", None)
    return jax.shard_map(local, mesh=mesh, in_specs=in_specs, out_specs=out_specs, check_vma=False)
```

profile of v0, /device:TPU:1, one launch (start us, length us, event | category | flops | bytes accessed | tf_op | source)
XLA Modules:
  0.0 229.7 jit_solution(12196940942636767293)
XLA Ops:
  6.5 0.8 reshape.223
  7.4 2.3 pad_maximum_fusion
  9.7 0.7 all-gather.5.cloned.1.call-update
  10.4 0.8 reduce-window.4
  11.4 0.7 fusion.48
  12.2 3.1 %fusion.12 = f32[128]{0:T(128)S(1)} fusion(bf16[1,128,16384]{2,1,0:T(8,128)(2,1)} %param.11), kind=kLoop, calls=%fused_computation.20 | loop fusion | flops 6291328 | bytes 4194816 | tf_op jit(solution)/shard_map/reduce_sum | solution.py:142
  15.3 0.2 multiply_cosine_fusion
  15.5 119.3 %all-gather.3.cloned.1.call-done = bf16[16384,513]{1,0:T(8,128)(2,1)} async-done(((bf16[512,513]{1,0:T(8,128)(2,1)}), bf16[16384,513]{1,0:T(8,128)(2,1)}) %all-gather.3.cloned.1.call-update) | async-done | bytes 16810000 | tf_op jit(solution)/shard_map/all_gather | solution.py:15
  134.9 3.0 %convert_reduce_fusion = f32[16384]{0:T(1024)S(1)} fusion(bf16[16384,513]{1,0:T(8,128)(2,1)} %all-gather.3.cloned.1.call-done), kind=kLoop, calls=%fused_computation.26 | loop fusion | flops 16384 | bytes 98304 | tf_op jit(solution)/shard_map/convert_element_type | solution.py:77
  137.9 8.3 %fusion.28 = f32[128,1,128]{0,2,1:T(8,128)S(1)} fusion(bf16[16384,513]{1,0:T(8,128)(2,1)} %all-gather.3.cloned.1.call-done, bf16[1,128,16384]{2,1,0:T(8,128)(2,1)} %param.11, f32[16384]{0:T(1024)S(1)} %convert_reduce_fusion, f32[128]{0:T(128)S(1)} %add_rsqrt_fusion), kind=kOutput, calls=%fused_computation.35 | convolution fusion | flops 545259520 | bytes 8520192 | tf_op jit(solution)/shard_map/dot_general | solution.py:80
  146.2 0.2 fusion.45
  146.5 7.2 %fusion.33 = bf16[128,128]{0,1:T(8,128)(2,1)S(1)} fusion(bf16[16384,513]{1,0:T(8,128)(2,1)} %all-gather.3.cloned.1.call-done, bf16[1,128,16384]{2,1,0:T(8,128)(2,1)S(1)} %copy-done, f32[16384]{0:T(1024)S(1)} %convert_reduce_fusion, f32[128]{0:T(128)S(1)} %add_rsqrt_fusion), kind=kOutput, calls=%fused_computation.36 | convolution fusion | flops 545275904 | bytes 8487424 | tf_op jit(solution)/shard_map/dot_general | solution.py:81
  153.8 0.8 broadcast_in_dim.23
  154.6 8.9 %all-to-all-start = ((bf16[8,128,256]{2,1,0:T(8,128)(2,1)}), bf16[8,128,256]{2,1,0:T(8,128)(2,1)S(1)}, u32[]{:S(2)}, u32[]{:S(2)}) async-start(bf16[8,128,256]{2,1,0:T(8,128)(2,1)} %broadcast_in_dim.23), calls=%async_computation | async-start | bytes 1048576 | tf_op jit(solution)/shard_map/all_to_all | solution.py:25
  163.5 9.9 %slice_bitcast_fusion = bf16[256,16384]{0,1:T(8,128)(2,1)} fusion(bf16[16384,513]{1,0:T(8,128)(2,1)} %all-gather.3.cloned.1.call-done), kind=kLoop, calls=%fused_computation.25 | loop fusion | bytes 16777216 | tf_op jit(solution)/shard_map/dot_general | solution.py:79
  173.4 12.0 %copy.21 = bf16[256,16384]{1,0:T(8,128)(2,1)} copy(bf16[256,16384]{0,1:T(8,128)(2,1)} %slice_bitcast_fusion) | data formatting | bytes 16777216 | tf_op jit(solution)/shard_map/dot_general | solution.py:79
  185.3 7.3 %fusion.18 = f32[128,2,128]{0,2,1:T(8,128)S(1)} fusion(bf16[2,128,16384]{2,1,0:T(8,128)(2,1)} %bitcast.68, bf16[1,128,16384]{2,1,0:T(8,128)(2,1)} %param.11, f32[16384]{0:T(1024)S(1)} %convert_reduce_fusion, f32[128]{0:T(128)S(1)} %add_rsqrt_fusion), kind=kOutput, calls=%fused_computation.28 | convolution fusion | flops 1082130432 | bytes 12780032 | tf_op jit(solution)/shard_map/dot_general | solution.py:79
  192.6 0.1 copy.22
  192.9 11.9 %while.17 = (s32[]{:T(128)}, f32[2,128,128]{2,1,0:T(8,128)S(1)}, f32[2,128]{1,0:T(2,128)S(1)}, s32[]{:T(128)}, s32[1024]{0:T(1024)S(1)}, /*index=5*/s32[128]{0:T...) while((s32[]{:T(128)}, f32[2,128,128]{2,1,0:T(8,128)S(1)}, ...), condition=%wide.region_8.9_spmd, body=%wide.region_4.8_spmd.sunk | while | flops 16957704 | bytes 567161 | solution.py:131
  193.0 0.6 slice.77
  194.2 0.6 conditional.2
  194.4 0.2 fusion.49
  194.6 0.2 convolution_add_fusion
  194.9 0.6 slice.77
  196.3 0.6 slice.77
  197.8 0.6 slice.77
  199.2 0.6 slice.77
  200.6 0.6 slice.77
  202.0 0.6 slice.77
  203.4 0.6 slice.77
  204.9 11.3 %all-gather.5.cloned.1.call-done = bf16[256,16384]{1,0:T(8,128)(2,1)} async-done(((bf16[256,512]{1,0:T(8,128)(2,1)}), bf16[256,16384]{1,0:T(8,128)(2,1)}) %all-gather.5.cloned.1.call-update) | async-done | bytes 8388624 | tf_op jit(solution)/shard_map/all_gather | solution.py:176
  216.2 6.7 %fusion.9 = bf16[1,128,16384]{2,1,0:T(8,128)(2,1)} fusion(bf16[128,256]{0,1:T(8,128)(2,1)S(1)} %bitcast.70, bf16[256,16384]{1,0:T(8,128)(2,1)} %all-gather.5.cloned.1.call-done), kind=kOutput, calls=%fused_computation.15 | convolution fusion | flops 1075838976 | bytes 12648448 | tf_op jit(solution)/shard_map/dot_general | solution.py:174
  (49 shorter events, 1.6 us)
Async XLA Ops:
  6.5 128.3 %all-gather.3.cloned.1.call-start = ((), (), s32[]{:S(2)}) async-start(), calls=%async_computation.1 | async-start | bytes 21626880 | tf_op jit(solution)/shard_map/all_gather | solution.py:15
  9.6 206.5 %all-gather.5.cloned.1.call-start = ((), (), s32[]{:S(2)}) async-start(), calls=%async_computation.2 | async-start | bytes 8650752 | tf_op jit(solution)/shard_map/all_gather | solution.py:176
  134.9 11.6 %copy-start = (bf16[1,128,16384]{2,1,0:T(8,128)(2,1)S(1)}, bf16[1,128,16384]{2,1,0:T(8,128)(2,1)}, u32[]{:S(2)}) copy-start(bf16[1,128,16384]{2,1,0:T(8,128)(2,1)} %param.11) | copy-start | bytes 12582916
  154.6 38.2 %all-to-all-start = ((bf16[8,128,256]{2,1,0:T(8,128)(2,1)}), bf16[8,128,256]{2,1,0:T(8,128)(2,1)S(1)}, u32[]{:S(2)}, u32[]{:S(2)}) async-start(bf16[8,128,256]{2,1,0:T(8,128)(2,1)} %broadcast_in_dim.23), calls=%async_computation | async-start | bytes 1048576 | tf_op jit(solution)/shard_map/all_to_all | solution.py:25
Sparse Core Ops, SparseCore 0:
  9.8 125.0 all-gather.2
  136.7 79.3 all-gather.4
where the time goes:
time: 230 us
  waiting for transfers between devices  131 us (57%)
  matrix products  29.8 us (13%)
  local copies, waits for them, and re-layouts  29.7 us (13%)
  between operations  13.6 us (6%)
  other arithmetic  10.7 us (5%)
  starting transfers between devices  8.9 us (4%)
  loops' own time  5.59 us (2%)
    all_gather x1, waiting for transfers between devices, side_by_side(): out, at, outs = (lax.all_gather(both, axis, axis=dim, tiled=True), 0, [])  119 us
    dot_general x2, local copies, waits for them, and re-layouts, fold_panels(): jnp.dot(normed, query_piece, preferred_element_type=jnp.float32)  21.9 us
    all_gather x1, waiting for transfers between devices, local(): lax.all_gather(out_weight, 'fsdp', axis=1, tiled=True)  11.3 us
    all_to_all x1, starting transfers between devices, copy_for_each(): lax.all_to_all(jnp.broadcast_to(array[None], (length, *array.shape)), axi...  8.86 us
    dot_general x1, matrix products, fold_panels(): jnp.dot(normed, key_piece, preferred_element_type=jnp.float32)  8.33 us
    dot_general x1, matrix products, fold_panels(): jnp.dot(normed, query_piece, preferred_element_type=jnp.float32)  7.26 us
    dot_general x1, matrix products, fold_panels(): jnp.dot(normed, value_piece, preferred_element_type=jnp.float32)  7.16 us
    dot_general x1, matrix products, local(): jnp.dot(attended, lax.all_gather(out_weight, 'fsdp', axis=1, tiled=True),...  6.69 us
  transfers between devices with their start and end apart: 3, of which 2 were waited for; matrix products, arithmetic and copies ran while one was open for 26% of the time, Pallas kernels for 0%

commit v1 on v0

--- a/solution.py
+++ b/solution.py
@@ -173,7 +173,9 @@
     attended = results[0]
     mixed = jnp.dot(
         attended,
-        lax.all_gather(out_weight, "fsdp", axis=1, tiled=True),
+        jnp.concatenate(
+            lax.all_to_all(jnp.stack([out_weight] * lax.axis_size("fsdp")), "fsdp", 0, 0), axis=1
+        ),
         preferred_element_type=jnp.float32,
     ).astype(jnp.bfloat16)
     return mixed[None, :, :]

time: 230 us -> 394 us (1.71)
  waiting for transfers between devices: 131 us -> 280 us
  starting transfers between devices: 8.9 us -> 18.5 us
  local copies, waits for them, and re-layouts: 29.7 us -> 33.8 us
    all_to_all x0 -> x1, waiting for transfers between devices: none -> 144 us  [local(): lax.all_to_all(jnp.stack([out_weight] * lax.axis_size('fsdp')), 'fsdp', 0...]
    all_to_all x1, waiting for transfers between devices: 0.01 us -> 15.3 us  [copy_for_each(): lax.all_to_all(jnp.broadcast_to(array[None], (length, *array.shape)), axi...]
    all_gather x1 -> x0, waiting for transfers between devices: 11.3 us -> none  [local(): lax.all_gather(out_weight, 'fsdp', axis=1, tiled=True)]
    all_to_all x0 -> x1, starting transfers between devices: none -> 9.56 us  [local(): lax.all_to_all(jnp.stack([out_weight] * lax.axis_size('fsdp')), 'fsdp', 0...]
    another operation x0 -> x1, local copies, waits for them, and re-layouts: none -> 4.27 us  [local(): jnp.stack([out_weight] * lax.axis_size('fsdp'))]
  transfers between devices with their start and end apart: 3 -> 3, of which waited for: 2 -> 3; matrix products, arithmetic and copies ran while one was open for 26% -> 10% of each run, Pallas kernels for 0% -> 0%
where the time goes in v1:
time: 394 us; the launch traced here: 393 us
  waiting for transfers between devices  280 us (71%)
  local copies, waits for them, and re-layouts  33.8 us (9%)
  matrix products  31 us (8%)
  starting transfers between devices  18.5 us (5%)
  between operations  13.6 us (3%)
  other arithmetic  10.7 us (3%)
  loops' own time  5.5 us (1%)
    all_to_all x1, waiting for transfers between devices, local(): lax.all_to_all(jnp.stack([out_weight] * lax.axis_size('fsdp')), 'fsdp', 0...  144 us
    all_gather x1, waiting for transfers between devices, side_by_side(): out, at, outs = (lax.all_gather(both, axis, axis=dim, tiled=True), 0, [])  120 us
    dot_general x2, local copies, waits for them, and re-layouts, fold_panels(): jnp.dot(normed, query_piece, preferred_element_type=jnp.float32)  21.8 us
    all_to_all x1, waiting for transfers between devices, copy_for_each(): lax.all_to_all(jnp.broadcast_to(array[None], (length, *array.shape)), axi...  15.3 us
    all_to_all x1, starting transfers between devices, local(): lax.all_to_all(jnp.stack([out_weight] * lax.axis_size('fsdp')), 'fsdp', 0...  9.56 us
    all_to_all x1, starting transfers between devices, copy_for_each(): lax.all_to_all(jnp.broadcast_to(array[None], (length, *array.shape)), axi...  8.97 us
    dot_general x1, matrix products, fold_panels(): jnp.dot(normed, key_piece, preferred_element_type=jnp.float32)  8.26 us
    dot_general x1, matrix products, local(): jnp.dot(attended, jnp.concatenate(lax.all_to_all(jnp.stack([out_weight] *...  8.23 us
  transfers between devices with their start and end apart: 3, of which 3 were waited for; matrix products, arithmetic and copies ran while one was open for 10% of the time, Pallas kernels for 0%

profile of v1, /device:TPU:1, one launch (start us, length us, event | category | flops | bytes accessed | tf_op | source)
XLA Modules:
  0.0 393.0 jit_solution(14187622417109735787)
XLA Ops:
  6.5 0.8 reshape.233
  7.4 2.3 pad_maximum_fusion
  9.6 0.8 reduce-window.4
  10.6 0.7 fusion.48
  11.4 3.1 fusion.12
  14.5 120.4 %all-gather.2.cloned.1.call-done = bf16[16384,513]{1,0:T(8,128)(2,1)} async-done(((bf16[512,513]{1,0:T(8,128)(2,1)}), bf16[16384,513]{1,0:T(8,128)(2,1)}) %all-gather.2.cloned.1.call-update) | async-done | bytes 16810000 | tf_op jit(solution)/shard_map/all_gather | solution.py:15
  134.9 3.0 convert_reduce_fusion
  137.9 8.3 %fusion.28 = f32[128,1,128]{0,2,1:T(8,128)S(1)} fusion(bf16[16384,513]{1,0:T(8,128)(2,1)} %all-gather.2.cloned.1.call-done, bf16[1,128,16384]{2,1,0:T(8,128)(2,1)} %param.11, f32[16384]{0:T(1024)S(1)} %convert_reduce_fusion, f32[128]{0:T(128)S(1)} %add_rsqrt_fusion), kind=kOutput, calls=%fused_computation.35 | convolution fusion | flops 545259520 | bytes 8520192 | tf_op jit(solution)/shard_map/dot_general | solution.py:80
  146.2 0.2 fusion.45
  146.4 7.0 %fusion.33 = bf16[128,128]{0,1:T(8,128)(2,1)S(1)} fusion(bf16[16384,513]{1,0:T(8,128)(2,1)} %all-gather.2.cloned.1.call-done, bf16[1,128,16384]{2,1,0:T(8,128)(2,1)S(1)} %copy-done, f32[16384]{0:T(1024)S(1)} %convert_reduce_fusion, f32[128]{0:T(128)S(1)} %add_rsqrt_fusion), kind=kOutput, calls=%fused_computation.36 | convolution fusion | flops 545275904 | bytes 8487424 | tf_op jit(solution)/shard_map/dot_general | solution.py:81
  153.6 0.8 broadcast_in_dim.23
  154.4 9.0 %all-to-all-start = ((bf16[8,128,256]{2,1,0:T(8,128)(2,1)}), bf16[8,128,256]{2,1,0:T(8,128)(2,1)S(1)}, u32[]{:S(2)}, u32[]{:S(2)}) async-start(bf16[8,128,256]{2,1,0:T(8,128)(2,1)} %broadcast_in_dim.23), calls=%async_computation | async-start | bytes 1048576 | tf_op jit(solution)/shard_map/all_to_all | solution.py:25
  163.5 15.3 %all-to-all-done = bf16[8,128,256]{2,1,0:T(8,128)(2,1)S(1)} async-done(((bf16[8,128,256]{2,1,0:T(8,128)(2,1)}), bf16[8,128,256]{2,1,0:T(8,128)(2,1)S(1)}, u32[]{:S(2)}, u32[]{:S(2)}) %all-to-all-start) | async-done | bytes 524320 | tf_op jit(solution)/shard_map/all_to_all | solution.py:25
  178.8 4.3 %stack.2 = bf16[32,256,512]{1,2,0:T(8,128)(2,1)} broadcast(bf16[256,512]{0,1:T(8,128)(2,1)S(1)} %copy.25), dimensions={1,2} | broadcast | bytes 8650752 | tf_op jit(solution)/shard_map/stack | solution.py:177
  183.1 9.6 %all-to-all-start.1 = ((bf16[32,256,512]{1,2,0:T(8,128)(2,1)}), bf16[32,256,512]{1,2,0:T(8,128)(2,1)}, u32[]{:S(2)}, u32[]{:S(2)}) async-start(bf16[32,256,512]{1,2,0:T(8,128)(2,1)} %stack.2), calls=%async_computation.1 | async-start | bytes 16777216 | tf_op jit(solution)/shard_map/all_to_all | solution.py:177
  192.9 9.8 %slice_bitcast_fusion = bf16[256,16384]{0,1:T(8,128)(2,1)} fusion(bf16[16384,513]{1,0:T(8,128)(2,1)} %all-gather.2.cloned.1.call-done), kind=kLoop, calls=%fused_computation.25 | loop fusion | bytes 16777216 | tf_op jit(solution)/shard_map/dot_general | solution.py:79
  202.7 12.0 %copy.22 = bf16[256,16384]{1,0:T(8,128)(2,1)} copy(bf16[256,16384]{0,1:T(8,128)(2,1)} %slice_bitcast_fusion) | data formatting | bytes 16777216 | tf_op jit(solution)/shard_map/dot_general | solution.py:79
  214.7 7.0 %fusion.18 = f32[128,2,128]{0,2,1:T(8,128)S(1)} fusion(bf16[2,128,16384]{2,1,0:T(8,128)(2,1)} %bitcast.71, bf16[1,128,16384]{2,1,0:T(8,128)(2,1)} %param.11, f32[16384]{0:T(1024)S(1)} %convert_reduce_fusion, f32[128]{0:T(128)S(1)} %add_rsqrt_fusion), kind=kOutput, calls=%fused_computation.28 | convolution fusion | flops 1082130432 | bytes 12780032 | tf_op jit(solution)/shard_map/dot_general | solution.py:79
  222.0 11.6 %while.17 = (s32[]{:T(128)}, f32[2,128,128]{2,1,0:T(8,128)S(1)}, f32[2,128]{1,0:T(2,128)S(1)}, s32[]{:T(128)}, s32[1024]{0:T(1024)S(1)}, /*index=5*/s32[128]{0:T...) while((s32[]{:T(128)}, f32[2,128,128]{2,1,0:T(8,128)S(1)}, ...), condition=%wide.region_8.9_spmd, body=%wide.region_4.8_spmd.sunk | while | flops 16957704 | bytes 567153 | solution.py:131
  222.1 0.6 slice.77
  223.3 0.6 conditional.2
  223.5 0.2 fusion.49
  223.7 0.2 convolution_add_fusion
  224.0 0.6 slice.77
  225.4 0.6 slice.77
  226.8 0.6 slice.77
  228.1 0.6 slice.77
  229.5 0.6 slice.77
  230.9 0.6 slice.77
  232.3 0.6 slice.77
  233.7 144.2 %all-to-all-done.1 = bf16[32,256,512]{1,2,0:T(8,128)(2,1)} async-done(((bf16[32,256,512]{1,2,0:T(8,128)(2,1)}), bf16[32,256,512]{1,2,0:T(8,128)(2,1)}, u32[]{:S(2)}, u32[]{:S(2)}) %all-to-all-start.1) | async-done | bytes 8388640 | tf_op jit(solution)/shard_map/all_to_all | solution.py:177
  377.9 8.2 %fusion.9 = bf16[1,128,16384]{2,1,0:T(8,128)(2,1)} fusion(bf16[128,256]{0,1:T(8,128)(2,1)S(1)} %bitcast.73, bf16[256,16384]{0,1:T(8,128)(2,1)} %bitcast.20), kind=kOutput, calls=%fused_computation.15 | convolution fusion | flops 1075838976 | bytes 12648448 | tf_op jit(solution)/shard_map/dot_general | solution.py:174
  (52 shorter events, 2.0 us)
Async XLA Ops:
  6.5 128.3 %all-gather.2.cloned.1.call-start = ((), (), s32[]{:S(2)}) async-start(), calls=%async_computation.2 | async-start | bytes 21626880 | tf_op jit(solution)/shard_map/all_gather | solution.py:15
  134.9 11.5 %copy-start = (bf16[1,128,16384]{2,1,0:T(8,128)(2,1)S(1)}, bf16[1,128,16384]{2,1,0:T(8,128)(2,1)}, u32[]{:S(2)}) copy-start(bf16[1,128,16384]{2,1,0:T(8,128)(2,1)} %param.11) | copy-start | bytes 12582916
  146.2 17.2 %copy-start.1 = (bf16[256,512]{1,0:T(8,128)(2,1)S(1)}, bf16[256,512]{1,0:T(8,128)(2,1)}, u32[]{:S(2)}) copy-start(bf16[256,512]{1,0:T(8,128)(2,1)} %param.16) | copy-start | bytes 786436
  154.4 24.4 %all-to-all-start = ((bf16[8,128,256]{2,1,0:T(8,128)(2,1)}), bf16[8,128,256]{2,1,0:T(8,128)(2,1)S(1)}, u32[]{:S(2)}, u32[]{:S(2)}) async-start(bf16[8,128,256]{2,1,0:T(8,128)(2,1)} %broadcast_in_dim.23), calls=%async_computation | async-start | bytes 1048576 | tf_op jit(solution)/shard_map/all_to_all | solution.py:25
  183.1 194.8 %all-to-all-start.1 = ((bf16[32,256,512]{1,2,0:T(8,128)(2,1)}), bf16[32,256,512]{1,2,0:T(8,128)(2,1)}, u32[]{:S(2)}, u32[]{:S(2)}) async-start(bf16[32,256,512]{1,2,0:T(8,128)(2,1)} %stack.2), calls=%async_computation.1 | async-start | bytes 16777216 | tf_op jit(solution)/shard_map/all_to_all | solution.py:177
Sparse Core Ops, SparseCore 0:
  9.8 125.0 all-gather.1
